TPU v7x, 512 devices: a whole 4x4x16 slice. The times are simulated.
512 devices in a mesh: row: 16 (over y, z_hi, core), col: 32 (over z_lo, x).
Axes of the slice: x: 4, y: 4, z: 16 (z_hi: 2, z_lo: 8; z = z_hi * 8 + z_lo), core: 2. Of those that a mesh axis runs over, the one named last changes fastest.
Arguments:
- images: bfloat16 [4096, 1024], P(('row', 'col')), may hold values from -6 to 6
- texts: bfloat16 [4096, 1024], P(('row', 'col')), may hold values from -6 to 6
- loss_weights: float32 [2], replicated, may hold values from 0.5 to 1.5
Outputs:
- grad_images: float32 [4096, 1024], P(('row', 'col'))
- grad_texts: float32 [4096, 1024], P(('row', 'col'))
All inputs are finite; a program needn't handle non-finite values.
Results may differ from a plain program's by a relative error of at most 0.0013.
Values may be sent and summed in bfloat16 or wider, within the bound.
A program may use at most 64 MiB of HBM per device.

v0:
```python
import math

import jax
import jax.numpy as jnp
from jax import lax
from jax.sharding import PartitionSpec as P


def local(images, texts, loss_weights):
    width = images.shape[1]
    batch = images.shape[0] * lax.axis_size("row") * lax.axis_size("col")
    scale = 1.0 / math.sqrt(width * batch)
    cross_scale = loss_weights[0] * scale
    inner_scale = loss_weights[1] * scale
    own = jnp.stack([images, texts])
    columns = lax.all_gather(own, "row", axis=1, tiled=True)
    col_img = columns[0]
    col_txt = columns[1]
    col_count = col_img.shape[0]
    keys = jnp.concatenate(
        [
            jnp.concatenate([col_txt, -col_img], axis=1),
            jnp.concatenate([col_img, -col_txt], axis=1),
        ],
        axis=0,
    )
    piece = lax.all_gather(own, "col", axis=1, tiled=True)
    joined = jnp.concatenate([piece[0], piece[1]], axis=1)
    scores = lax.dot_general(
        joined, keys, (((1,), (1,)), ((), ())), preferred_element_type=jnp.float32
    )
    p_mat = (scores[:, :col_count] * cross_scale).astype(jnp.bfloat16)
    q_mat = (scores[:, col_count:] * inner_scale).astype(jnp.bfloat16)
    joined, weights = (joined, jnp.concatenate([p_mat, q_mat], axis=1))
    result = jnp.dot(weights, keys, preferred_element_type=jnp.float32)
    terms = jnp.stack([result[:, :width], result[:, width:]])
    grads = lax.psum_scatter(terms, "col", scatter_dimension=1, tiled=True)
    return (grads[0], grads[1])


def solution(mesh):
    in_specs = (P(("row", "col"), None), P(("row", "col"), None), P())
    out_specs = (P(("row", "col"), None), P(("row", "col"), None))
    return jax.shard_map(local, mesh=mesh, in_specs=in_specs, out_specs=out_specs, check_vma=False)
```

profile of v0, /device:TPU:8, one launch (start us, length us, event | category | flops | bytes accessed | tf_op | source)
XLA Modules:
  0.0 497.0 jit_solution(4307591087020093460)
XLA Ops:
  7.2 0.0 all-gather.2.cloned.1.call-start
  7.2 1.4 pad_maximum_fusion.1
  8.6 0.0 all-gather.2.cloned.1.call-update
  8.6 0.0 reduce-scatter.2.cloned.1.call-start
  8.6 1.3 fusion.14
  11.2 54.2 %all_gather.7 = bf16[2,128,1024]{2,1,0:T(8,128)(2,1)S(1)} all-gather(bf16[2,8,1024]{2,1,0:T(8,128)(2,1)} %pad_maximum_fusion.1), channel_id=1, replica_groups=mesh['row'=16,'col'=32] {'row'}, dimensions={1}, use_global_device_ids=true | all-gather | bytes 557056 | tf_op jit(solution)/shard_map/all_gather | solution.py:16
  65.5 173.2 %all-gather.2.cloned.1.call-done = bf16[2,256,1024]{2,1,0:T(8,128)(2,1)} async-done(((bf16[2,8,1024]{2,1,0:T(8,128)(2,1)}), bf16[2,256,1024]{2,1,0:T(8,128)(2,1)}) %all-gather.2.cloned.1.call-update) | async-done | bytes 1048592 | tf_op jit(solution)/shard_map/all_gather | solution.py:27
  238.6 1.3 slice_bitcast_fusion.3
  239.9 0.6 fusion
  240.5 0.5 fusion.4
  241.0 0.2 slice_bitcast_fusion.1
  241.2 1.5 pad_maximum_fusion
  242.7 0.0 reduce-scatter.2.cloned.1.call-update
  242.7 246.1 %reduce-scatter.2.cloned.1.call-done = f32[2,8,1024]{2,1,0:T(8,128)} async-done(((f32[2,256,1024]{2,1,0:T(8,128)}), f32[2,8,1024]{2,1,0:T(8,128)}) %reduce-scatter.2.cloned.1.call-update) | async-done | bytes 65552 | tf_op jit(solution)/shard_map/reduce_scatter | solution.py:37
  488.8 1.4 slice_bitcast_fusion.6
  (3 shorter events, 0.1 us)
Async XLA Ops:
  7.2 231.5 %all-gather.2.cloned.1.call-start = ((), (), s32[]{:S(2)}) async-start(), calls=%async_computation.1 | async-start | bytes 1081344 | tf_op jit(solution)/shard_map/all_gather | solution.py:27
  8.6 480.2 %reduce-scatter.2.cloned.1.call-start = ((), (), s32[]{:S(2)}) async-start(), calls=%async_computation.2 | async-start | bytes 2162688 | tf_op jit(solution)/shard_map/reduce_scatter | solution.py:37
Sparse Core Ops, SparseCore 0:
  10.6 227.9 all-gather.1
  242.8 245.9 reduce-scatter.1
where the time goes:
time: 497 us
  waiting for transfers between devices  419 us (84%)
  blocking collectives  54.2 us (11%)
  between operations  15.3 us (3%)
    reduce_scatter x1, waiting for transfers between devices, local(): grads = lax.psum_scatter(terms, 'col', scatter_dimension=1, tiled=True)  246 us
    all_gather x1, waiting for transfers between devices, local(): piece = lax.all_gather(own, 'col', axis=1, tiled=True)  173 us
    all_gather x1, blocking collectives, local(): columns = lax.all_gather(own, 'row', axis=1, tiled=True)  54.2 us
  transfers between devices with their start and end apart: 2, of which 2 were waited for; matrix products, arithmetic and copies ran while one was open for 0% of the time, Pallas kernels for 0%

commit v1 on v0

v1 whole, which is shorter than its diff:
```python
import functools
import math

import jax
import jax.numpy as jnp
from jax import lax
from jax.experimental import pallas as pl
from jax.experimental.pallas import tpu as pltpu
from jax.sharding import PartitionSpec as P

MESH = pl.DeviceIdType.MESH
NX, NY, NZ, CORES = 4, 4, 16, 2
HALF = NZ // 2


def ring_distance(step, size):
    return min(step, size - step)


PLANE = sorted(
    [(dx, dy) for dy in range(NY) for dx in range(NX)],
    key=lambda o: -(ring_distance(o[0], NX) + ring_distance(o[1], NY)),
)
PEERS = len(PLANE) - 1


def kernel(scale, weights, img, txt, out, xi, xj, w, part, inbox, up_send, up_recv, down_send, down_recv, sib_send, sib_recv, i_send, i_recv, g_send, g_recv):
    rows, width = xi.shape[1:]
    half = width // 2
    row, col = lax.axis_index("row"), lax.axis_index("col")
    y, zh, core = row // 4, (row // 2) % 2, row % 2
    zl, x = col // NX, col % NX
    z = zh * 8 + zl

    def device(x, y, z, core):
        return (y * 4 + (z // 8) * 2 + core, (z % 8) * NX + x)

    above = device(x, y, (z + 1) % NZ, core)
    below = device(x, y, (z + NZ - 1) % NZ, core)
    sibling = device(x, y, z, 1 - core)
    ahead = [device((x + dx) % NX, (y + dy) % NY, z, core) for dx, dy in PLANE[:PEERS]]
    behind = [device((x + NX - dx) % NX, (y + NY - dy) % NY, z, core) for dx, dy in PLANE[:PEERS]]

    own = jnp.concatenate([img[...].astype(jnp.float32), txt[...].astype(jnp.float32)], axis=0).astype(jnp.bfloat16)
    xj[0] = own
    xi[PEERS] = own

    barrier = pltpu.get_barrier_semaphore()
    for peer in [above, below, sibling] + ahead:
        pl.semaphore_signal(barrier, inc=1, device_id=peer, device_id_type=MESH)
    pl.semaphore_wait(barrier, 3 + PEERS)

    def piece(slot, h):
        return xj.at[slot, :, pl.ds(h * half, half)]

    def hop(up, d, h):
        src, dst = (d - 1, d) if up else ((NZ - d + 1) % NZ, NZ - d)
        send, recv = (up_send, up_recv) if up else (down_send, down_recv)
        return pltpu.make_async_remote_copy(
            src_ref=piece(src, h), dst_ref=piece(dst, h), send_sem=send.at[d - 1, h], recv_sem=recv.at[d - 1, h],
            device_id=above if up else below, device_id_type=MESH)

    def across(slot, h):
        return pltpu.make_async_remote_copy(
            src_ref=piece(slot, h), dst_ref=piece(slot + NZ, h), send_sem=sib_send.at[slot, h], recv_sem=sib_recv.at[slot, h],
            device_id=sibling, device_id_type=MESH)

    def spread(k):
        return pltpu.make_async_remote_copy(
            src_ref=xi.at[PEERS], dst_ref=xi.at[k], send_sem=i_send.at[k], recv_sem=i_recv.at[k],
            device_id=ahead[k], device_id_type=MESH)

    def give(k):
        return pltpu.make_async_remote_copy(
            src_ref=part.at[k], dst_ref=inbox.at[k], send_sem=g_send.at[k], recv_sem=g_recv.at[k],
            device_id=behind[k], device_id_type=MESH)

    def moves(d):
        listed = [(True, 0), (False, 1)]
        if d < HALF:
            listed += [(True, 1), (False, 0)]
        return listed

    for up, h in moves(1):
        hop(up, 1, h).start()
    for h in range(2):
        across(0, h).start()
    for k in range(PEERS):
        spread(k).start()
    for d in range(1, HALF + 1):
        for up, h in moves(d):
            hop(up, d, h).wait_recv()
            if d < HALF and (up, h) in moves(d + 1):
                hop(up, d + 1, h).start()
            across(d if up else NZ - d, h).start()
    for k in range(PEERS):
        spread(k).wait_recv()
    for slot in range(NZ):
        for h in range(2):
            across(slot, h).wait_recv()

    blocks = PEERS + 1
    keys = xj[...].reshape(2 * NZ * rows, width)
    scores = lax.dot_general(
        xi[...].reshape(blocks * rows, width), keys, (((1,), (1,)), ((), ())), preferred_element_type=jnp.float32)
    lanes = scores.shape[1]
    lane_kind = (lax.broadcasted_iota(jnp.int32, scores.shape, 1) // 8) % 2
    row_kind = (lax.broadcasted_iota(jnp.int32, scores.shape, 0) // 8) % 2
    turned = jnp.where(lane_kind == 0, pltpu.roll(scores, lanes - 8, 1), pltpu.roll(scores, 8, 1))
    turned = turned.reshape(blocks, 2, 8, lanes)
    turned = jnp.concatenate([turned[:, 1:], turned[:, :1]], axis=1).reshape(scores.shape)
    factor = jnp.where(lane_kind == row_kind, weights[1] * scale, weights[0] * scale)
    w[...] = ((scores - turned) * factor).astype(jnp.bfloat16)

    group = 4
    for first in range(0, blocks, group):
        total = jnp.dot(w[pl.ds(first * rows, group * rows), :], keys, preferred_element_type=jnp.float32)
        for k in range(first, first + group):
            block = total[(k - first) * rows : (k - first + 1) * rows]
            if k < PEERS:
                part[k] = block.astype(jnp.bfloat16)
                give(k).start()
            else:
                mine = block
    for k in range(PEERS):
        give(k).wait_recv()
        mine = mine + inbox[k].astype(jnp.float32)
    out[0] = mine[:8]
    out[1] = mine[8:]

    for d in range(1, HALF + 1):
        for up, h in moves(d):
            hop(up, d, h).wait_send()
    for slot in range(NZ):
        for h in range(2):
            across(slot, h).wait_send()
    for k in range(PEERS):
        spread(k).wait_send()
        give(k).wait_send()


def local(images, texts, loss_weights):
    count, width = images.shape
    batch = count * lax.axis_size("row") * lax.axis_size("col")
    scale = 1.0 / math.sqrt(width * batch)
    rows = 2 * count
    dma = pltpu.SemaphoreType.DMA
    grads = pl.pallas_call(
        functools.partial(kernel, scale),
        out_shape=jax.ShapeDtypeStruct((2, count, width), jnp.float32),
        in_specs=[pl.BlockSpec(memory_space=pltpu.SMEM)] + [pl.BlockSpec(memory_space=pltpu.VMEM)] * 2,
        out_specs=pl.BlockSpec(memory_space=pltpu.VMEM),
        scratch_shapes=[
            pltpu.VMEM((PEERS + 1, rows, width), jnp.bfloat16),
            pltpu.VMEM((2 * NZ, rows, width), jnp.bfloat16),
            pltpu.VMEM(((PEERS + 1) * rows, 2 * NZ * rows), jnp.bfloat16),
            pltpu.VMEM((PEERS, rows, width), jnp.bfloat16),
            pltpu.VMEM((PEERS, rows, width), jnp.bfloat16),
            dma((HALF, 2)), dma((HALF, 2)), dma((HALF, 2)), dma((HALF, 2)),
            dma((NZ, 2)), dma((NZ, 2)),
            dma((PEERS,)), dma((PEERS,)), dma((PEERS,)), dma((PEERS,)),
        ],
        compiler_params=pltpu.CompilerParams(collective_id=0, has_side_effects=True, vmem_limit_bytes=32 * 1024 * 1024),
    )(loss_weights, images, texts)
    return (grads[0], grads[1])


def solution(mesh):
    in_specs = (P(("row", "col"), None), P(("row", "col"), None), P())
    out_specs = (P(("row", "col"), None), P(("row", "col"), None))
    return jax.shard_map(local, mesh=mesh, in_specs=in_specs, out_specs=out_specs, check_vma=False)
```

time: 497 us -> 54.8 us (0.11)
  the two profiles are of different devices: /device:TPU:8 before, /device:TPU:1 now
where the time goes in v1:
time: 54.8 us; the launch traced here: 54.5 us
  Pallas kernels  51.1 us (93%)
  local copies, waits for them, and re-layouts  2.71 us (5%)
  between operations  0.65 us (1%)
    pallas_call x1, Pallas kernels, local(): pl.pallas_call(functools.partial(kernel, scale), out_shape=jax.ShapeDtype...  51.1 us
    unnamed x6, local copies, waits for them, and re-layouts  2.08 us

profile of v1, /device:TPU:1, one launch (start us, length us, event | category | flops | bytes accessed | tf_op | source)
XLA Modules:
  0.0 54.5 jit_solution(10358953084157608850)
XLA Ops:
  0.6 0.0 copy-start
  0.6 0.7 %copy-done = bf16[8,1024]{1,0:T(8,128)(2,1)S(1)} copy-done((bf16[8,1024]{1,0:T(8,128)(2,1)S(1)}, bf16[8,1024]{1,0:T(8,128)(2,1)}, u32[]{:S(2)}) %copy-start) | copy-done | bytes 16408
  1.3 0.0 copy-start.1
  1.4 0.7 %copy-done.1 = bf16[8,1024]{1,0:T(8,128)(2,1)S(1)} copy-done((bf16[8,1024]{1,0:T(8,128)(2,1)S(1)}, bf16[8,1024]{1,0:T(8,128)(2,1)}, u32[]{:S(2)}) %copy-start.1) | copy-done | bytes 16408
  2.1 0.0 copy-start.2
  2.1 0.7 %copy-done.2 = f32[2]{0:T(128)S(1)} copy-done((f32[2]{0:T(128)S(1)}, f32[2]{0:T(128)}, u32[]{:S(2)}) %copy-start.2) | copy-done | bytes 32
  2.7 51.1 %shard_map.50 = f32[2,8,1024]{2,1,0:T(8,128)S(1)} custom-call(f32[2]{0:T(128)S(1)} %copy-done.2, bf16[8,1024]{1,0:T(8,128)(2,1)S(1)} %copy-done, bf16[8,1024]{1,0:T(8,128)(2,1)S(1)} %copy-done.1), custom_call_target="tpu_custom_call" | custom-call | tf_op jit(solution)/shard_map/pallas_call | solution.py:148
  53.9 0.6 %slice_bitcast_fusion = (f32[8,1024]{1,0:T(8,128)}, f32[8,1024]{1,0:T(8,128)}) fusion(f32[2,8,1024]{2,1,0:T(8,128)S(1)} %shard_map.50), kind=kLoop, calls=%fused_computation | loop fusion | bytes 131072 | tf_op jit(solution)/shard_map/squeeze | solution.py:165
Async XLA Ops:
  0.6 0.7 %copy-start = (bf16[8,1024]{1,0:T(8,128)(2,1)S(1)}, bf16[8,1024]{1,0:T(8,128)(2,1)}, u32[]{:S(2)}) copy-start(bf16[8,1024]{1,0:T(8,128)(2,1)} %img.1) | copy-start | bytes 49156
  1.3 0.7 %copy-start.1 = (bf16[8,1024]{1,0:T(8,128)(2,1)S(1)}, bf16[8,1024]{1,0:T(8,128)(2,1)}, u32[]{:S(2)}) copy-start(bf16[8,1024]{1,0:T(8,128)(2,1)} %txt.1) | copy-start | bytes 49156
  2.1 0.7 %copy-start.2 = (f32[2]{0:T(128)S(1)}, f32[2]{0:T(128)}, u32[]{:S(2)}) copy-start(f32[2]{0:T(128)} %weights.1) | copy-start | bytes 28

commit v2 on v1

--- a/solution.py
+++ b/solution.py
@@ -23,8 +23,13 @@
 )
 PEERS = len(PLANE) - 1
 
+NEAR = [(0, 5), (0, 2), (0, 1), (2, 1), (5, 3), (5, 2), (5, 1), (5, -1)]
+HOPS = [hop for origin, step in NEAR for hop in ((origin, step), (-origin, -step))]
+LINE_PEERS = sorted({step for _, step in HOPS})
+ARRIVALS = [hop for origin, step in [(0, 2), (0, 5), (0, 1), (2, 1), (5, 1), (5, -1), (5, 2), (5, 3)] for hop in ((origin, step), (-origin, -step))]
 
-def kernel(scale, weights, img, txt, out, xi, xj, w, part, inbox, up_send, up_recv, down_send, down_recv, sib_send, sib_recv, i_send, i_recv, g_send, g_recv):
+
+def kernel(scale, weights_hbm, img_hbm, txt_hbm, out, weights, img, txt, xi, xj, w, part, inbox, load_sem, z_send, z_recv, sib_send, sib_recv, i_send, i_recv, g_send, g_recv):
     rows, width = xi.shape[1:]
     half = width // 2
     row, col = lax.axis_index("row"), lax.axis_index("col")
@@ -35,34 +40,40 @@
     def device(x, y, z, core):
         return (y * 4 + (z // 8) * 2 + core, (z % 8) * NX + x)
 
-    above = device(x, y, (z + 1) % NZ, core)
-    below = device(x, y, (z + NZ - 1) % NZ, core)
     sibling = device(x, y, z, 1 - core)
+    line = {d: device(x, y, (z + d + NZ) % NZ, core) for d in LINE_PEERS}
     ahead = [device((x + dx) % NX, (y + dy) % NY, z, core) for dx, dy in PLANE[:PEERS]]
     behind = [device((x + NX - dx) % NX, (y + NY - dy) % NY, z, core) for dx, dy in PLANE[:PEERS]]
 
+    barrier = pltpu.get_barrier_semaphore()
+    for peer in list(line.values()) + [sibling] + ahead:
+        pl.semaphore_signal(barrier, inc=1, device_id=peer, device_id_type=MESH)
+
+    loads = [
+        pltpu.make_async_copy(img_hbm, img, load_sem.at[0]),
+        pltpu.make_async_copy(txt_hbm, txt, load_sem.at[1]),
+        pltpu.make_async_copy(weights_hbm, weights, load_sem.at[2]),
+    ]
+    for load in loads:
+        load.start()
+    for load in loads:
+        load.wait()
     own = jnp.concatenate([img[...].astype(jnp.float32), txt[...].astype(jnp.float32)], axis=0).astype(jnp.bfloat16)
     xj[0] = own
     xi[PEERS] = own
+    pl.semaphore_wait(barrier, len(line) + 1 + PEERS)
 
-    barrier = pltpu.get_barrier_semaphore()
-    for peer in [above, below, sibling] + ahead:
-        pl.semaphore_signal(barrier, inc=1, device_id=peer, device_id_type=MESH)
-    pl.semaphore_wait(barrier, 3 + PEERS)
+    def hop(origin, step):
+        src, dst = origin % NZ, (origin + step) % NZ
+        k = HOPS.index((origin, step))
+        part = slice(None) if dst != HALF else pl.ds(0 if step > 0 else half, half)
+        return pltpu.make_async_remote_copy(
+            src_ref=xj.at[src, :, part], dst_ref=xj.at[dst, :, part], send_sem=z_send.at[k], recv_sem=z_recv.at[k],
+            device_id=line[step], device_id_type=MESH)
 
-    def piece(slot, h):
-        return xj.at[slot, :, pl.ds(h * half, half)]
-
-    def hop(up, d, h):
-        src, dst = (d - 1, d) if up else ((NZ - d + 1) % NZ, NZ - d)
-        send, recv = (up_send, up_recv) if up else (down_send, down_recv)
+    def across(slot):
         return pltpu.make_async_remote_copy(
-            src_ref=piece(src, h), dst_ref=piece(dst, h), send_sem=send.at[d - 1, h], recv_sem=recv.at[d - 1, h],
-            device_id=above if up else below, device_id_type=MESH)
-
-    def across(slot, h):
-        return pltpu.make_async_remote_copy(
-            src_ref=piece(slot, h), dst_ref=piece(slot + NZ, h), send_sem=sib_send.at[slot, h], recv_sem=sib_recv.at[slot, h],
+            src_ref=xj.at[slot], dst_ref=xj.at[slot + NZ], send_sem=sib_send.at[slot], recv_sem=sib_recv.at[slot],
             device_id=sibling, device_id_type=MESH)
 
     def spread(k):
@@ -75,29 +86,25 @@
             src_ref=part.at[k], dst_ref=inbox.at[k], send_sem=g_send.at[k], recv_sem=g_recv.at[k],
             device_id=behind[k], device_id_type=MESH)
 
-    def moves(d):
-        listed = [(True, 0), (False, 1)]
-        if d < HALF:
-            listed += [(True, 1), (False, 0)]
-        return listed
-
-    for up, h in moves(1):
-        hop(up, 1, h).start()
-    for h in range(2):
-        across(0, h).start()
+    for origin, step in HOPS:
+        if origin == 0:
+            hop(0, step).start()
+    across(0).start()
     for k in range(PEERS):
         spread(k).start()
-    for d in range(1, HALF + 1):
-        for up, h in moves(d):
-            hop(up, d, h).wait_recv()
-            if d < HALF and (up, h) in moves(d + 1):
-                hop(up, d + 1, h).start()
-            across(d if up else NZ - d, h).start()
+    for origin, step in ARRIVALS:
+        hop(origin, step).wait_recv()
+        here = origin + step
+        for onward in HOPS:
+            if onward[0] == here:
+                hop(*onward).start()
+        if abs(here) != HALF:
+            across(here % NZ).start()
+    across(HALF).start()
     for k in range(PEERS):
         spread(k).wait_recv()
     for slot in range(NZ):
-        for h in range(2):
-            across(slot, h).wait_recv()
+        across(slot).wait_recv()
 
     blocks = PEERS + 1
     keys = xj[...].reshape(2 * NZ * rows, width)
@@ -128,12 +135,10 @@
     out[0] = mine[:8]
     out[1] = mine[8:]
 
-    for d in range(1, HALF + 1):
-        for up, h in moves(d):
-            hop(up, d, h).wait_send()
+    for origin, step in HOPS:
+        hop(origin, step).wait_send()
     for slot in range(NZ):
-        for h in range(2):
-            across(slot, h).wait_send()
+        across(slot).wait_send()
     for k in range(PEERS):
         spread(k).wait_send()
         give(k).wait_send()
@@ -148,19 +153,23 @@
     grads = pl.pallas_call(
         functools.partial(kernel, scale),
         out_shape=jax.ShapeDtypeStruct((2, count, width), jnp.float32),
-        in_specs=[pl.BlockSpec(memory_space=pltpu.SMEM)] + [pl.BlockSpec(memory_space=pltpu.VMEM)] * 2,
+        in_specs=[pl.BlockSpec(memory_space=pl.ANY)] * 3,
         out_specs=pl.BlockSpec(memory_space=pltpu.VMEM),
         scratch_shapes=[
+            pltpu.SMEM((2,), jnp.float32),
+            pltpu.VMEM((count, width), jnp.bfloat16),
+            pltpu.VMEM((count, width), jnp.bfloat16),
             pltpu.VMEM((PEERS + 1, rows, width), jnp.bfloat16),
             pltpu.VMEM((2 * NZ, rows, width), jnp.bfloat16),
             pltpu.VMEM(((PEERS + 1) * rows, 2 * NZ * rows), jnp.bfloat16),
             pltpu.VMEM((PEERS, rows, width), jnp.bfloat16),
             pltpu.VMEM((PEERS, rows, width), jnp.bfloat16),
-            dma((HALF, 2)), dma((HALF, 2)), dma((HALF, 2)), dma((HALF, 2)),
-            dma((NZ, 2)), dma((NZ, 2)),
+            dma((3,)),
+            dma((len(HOPS),)), dma((len(HOPS),)),
+            dma((NZ,)), dma((NZ,)),
             dma((PEERS,)), dma((PEERS,)), dma((PEERS,)), dma((PEERS,)),
         ],
-        compiler_params=pltpu.CompilerParams(collective_id=0, has_side_effects=True, vmem_limit_bytes=32 * 1024 * 1024),
+        compiler_params=pltpu.CompilerParams(collective_id=0, has_side_effects=True),
     )(loss_weights, images, texts)
     return (grads[0], grads[1])
 

time: 54.8 us -> 43 us (0.78)
  Pallas kernels: 51.1 us -> 40.7 us
  local copies, waits for them, and re-layouts: 2.71 us -> 1.4 us
    pallas_call x1, Pallas kernels: 51.1 us -> 40.7 us  [local(): pl.pallas_call(functools.partial(kernel, scale), out_shape=jax.ShapeDtype...]
    unnamed x6 -> x0, local copies, waits for them, and re-layouts: 2.08 us -> none
    squeeze x1, local copies, waits for them, and re-layouts: 0.63 us -> 1.4 us  [local(): return (grads[0], grads[1])]
where the time goes in v2:
time: 43 us; the launch traced here: 42.7 us
  Pallas kernels  40.7 us (95%)
  local copies, waits for them, and re-layouts  1.4 us (3%)
  between operations  0.64 us (1%)
    pallas_call x1, Pallas kernels, local(): pl.pallas_call(functools.partial(kernel, scale), out_shape=jax.ShapeDtype...  40.7 us
    squeeze x1, local copies, waits for them, and re-layouts, local(): return (grads[0], grads[1])  1.4 us

profile of v2, /device:TPU:1, one launch (start us, length us, event | category | flops | bytes accessed | tf_op | source)
XLA Modules:
  0.0 42.7 jit_solution(9264298753733959106)
XLA Ops:
  0.6 40.7 %shard_map.50 = f32[2,8,1024]{2,1,0:T(8,128)} custom-call(f32[2]{0:T(128)} %weights_hbm.1, bf16[8,1024]{1,0:T(8,128)(2,1)} %img_hbm.1, bf16[8,1024]{1,0:T(8,128)(2,1)} %txt_hbm.1), custom_call_target="tpu_custom_call" | custom-call | tf_op jit(solution)/shard_map/pallas_call | solution.py:153
  41.3 1.4 %slice_bitcast_fusion = (f32[8,1024]{1,0:T(8,128)}, f32[8,1024]{1,0:T(8,128)}) fusion(f32[2,8,1024]{2,1,0:T(8,128)} %shard_map.50), kind=kLoop, calls=%fused_computation | loop fusion | bytes 131072 | tf_op jit(solution)/shard_map/squeeze | solution.py:174

commit v3 on v2

--- a/solution.py
+++ b/solution.py
@@ -26,10 +26,13 @@
 NEAR = [(0, 5), (0, 2), (0, 1), (2, 1), (5, 3), (5, 2), (5, 1), (5, -1)]
 HOPS = [hop for origin, step in NEAR for hop in ((origin, step), (-origin, -step))]
 LINE_PEERS = sorted({step for _, step in HOPS})
-ARRIVALS = [hop for origin, step in [(0, 2), (0, 5), (0, 1), (2, 1), (5, 1), (5, -1), (5, 2), (5, 3)] for hop in ((origin, step), (-origin, -step))]
+ARRIVALS = [[(0, 2)], [(0, -2)], [(0, 5)], [(0, -5)]] + [
+    [(origin, step), (-origin, -step)] for origin, step in [(0, 1), (2, 1), (5, 1), (5, -1), (5, 2), (5, 3)]
+]
+GROUPS = [group[0] for group in ARRIVALS]
 
 
-def kernel(scale, weights_hbm, img_hbm, txt_hbm, out, weights, img, txt, xi, xj, w, part, inbox, load_sem, z_send, z_recv, sib_send, sib_recv, i_send, i_recv, g_send, g_recv):
+def kernel(scale, weights_hbm, img_hbm, txt_hbm, out, weights, own, xi, xj, w, part, inbox, load_sem, z_send, z_recv, sib_send, sib_recv, i_send, i_recv, g_send, g_recv):
     rows, width = xi.shape[1:]
     half = width // 2
     row, col = lax.axis_index("row"), lax.axis_index("col")
@@ -50,41 +53,44 @@
         pl.semaphore_signal(barrier, inc=1, device_id=peer, device_id_type=MESH)
 
     loads = [
-        pltpu.make_async_copy(img_hbm, img, load_sem.at[0]),
-        pltpu.make_async_copy(txt_hbm, txt, load_sem.at[1]),
+        pltpu.make_async_copy(img_hbm, own.at[0], load_sem.at[0]),
+        pltpu.make_async_copy(txt_hbm, own.at[1], load_sem.at[1]),
         pltpu.make_async_copy(weights_hbm, weights, load_sem.at[2]),
     ]
     for load in loads:
         load.start()
     for load in loads:
         load.wait()
-    own = jnp.concatenate([img[...].astype(jnp.float32), txt[...].astype(jnp.float32)], axis=0).astype(jnp.bfloat16)
-    xj[0] = own
-    xi[PEERS] = own
+    block = own[...].astype(jnp.float32).reshape(rows, width).astype(jnp.bfloat16)
+    xj[0] = block
+    xi[PEERS] = block
     pl.semaphore_wait(barrier, len(line) + 1 + PEERS)
 
     def hop(origin, step):
         src, dst = origin % NZ, (origin + step) % NZ
-        k = HOPS.index((origin, step))
+        k = GROUPS.index((origin, step)) if (origin, step) in GROUPS else GROUPS.index((-origin, -step))
         part = slice(None) if dst != HALF else pl.ds(0 if step > 0 else half, half)
         return pltpu.make_async_remote_copy(
-            src_ref=xj.at[src, :, part], dst_ref=xj.at[dst, :, part], send_sem=z_send.at[k], recv_sem=z_recv.at[k],
+            src_ref=xj.at[src, :, part], dst_ref=xj.at[dst, :, part], send_sem=z_send, recv_sem=z_recv.at[k],
             device_id=line[step], device_id_type=MESH)
 
     def across(slot):
         return pltpu.make_async_remote_copy(
-            src_ref=xj.at[slot], dst_ref=xj.at[slot + NZ], send_sem=sib_send.at[slot], recv_sem=sib_recv.at[slot],
+            src_ref=xj.at[slot], dst_ref=xj.at[slot + NZ], send_sem=sib_send, recv_sem=sib_recv,
             device_id=sibling, device_id_type=MESH)
 
     def spread(k):
         return pltpu.make_async_remote_copy(
-            src_ref=xi.at[PEERS], dst_ref=xi.at[k], send_sem=i_send.at[k], recv_sem=i_recv.at[k],
+            src_ref=xi.at[PEERS], dst_ref=xi.at[k], send_sem=i_send, recv_sem=i_recv,
             device_id=ahead[k], device_id_type=MESH)
 
     def give(k):
         return pltpu.make_async_remote_copy(
-            src_ref=part.at[k], dst_ref=inbox.at[k], send_sem=g_send.at[k], recv_sem=g_recv.at[k],
+            src_ref=part.at[k], dst_ref=inbox.at[k], send_sem=g_send, recv_sem=g_recv,
             device_id=behind[k], device_id_type=MESH)
+
+    def landed(ref, sem):
+        pltpu.make_async_copy(ref, ref, sem).wait()
 
     for origin, step in HOPS:
         if origin == 0:
@@ -92,19 +98,18 @@
     across(0).start()
     for k in range(PEERS):
         spread(k).start()
-    for origin, step in ARRIVALS:
-        hop(origin, step).wait_recv()
-        here = origin + step
-        for onward in HOPS:
-            if onward[0] == here:
-                hop(*onward).start()
-        if abs(here) != HALF:
-            across(here % NZ).start()
+    for group in ARRIVALS:
+        landed(xj.at[pl.ds(0, len(group))] if group[0] != (5, 3) else xj.at[0], z_recv.at[GROUPS.index(group[0])])
+        for origin, step in group:
+            here = origin + step
+            for onward in HOPS:
+                if onward[0] == here:
+                    hop(*onward).start()
+            if abs(here) != HALF:
+                across(here % NZ).start()
     across(HALF).start()
-    for k in range(PEERS):
-        spread(k).wait_recv()
-    for slot in range(NZ):
-        across(slot).wait_recv()
+    landed(xi.at[pl.ds(0, PEERS)], i_recv)
+    landed(xj.at[pl.ds(NZ, NZ)], sib_recv)
 
     blocks = PEERS + 1
     keys = xj[...].reshape(2 * NZ * rows, width)
@@ -129,19 +134,16 @@
                 give(k).start()
             else:
                 mine = block
+    landed(inbox, g_recv)
     for k in range(PEERS):
-        give(k).wait_recv()
         mine = mine + inbox[k].astype(jnp.float32)
     out[0] = mine[:8]
     out[1] = mine[8:]
 
-    for origin, step in HOPS:
-        hop(origin, step).wait_send()
-    for slot in range(NZ):
-        across(slot).wait_send()
-    for k in range(PEERS):
-        spread(k).wait_send()
-        give(k).wait_send()
+    landed(xj.at[pl.ds(0, NZ - 1)], z_send)
+    landed(xj.at[pl.ds(0, NZ)], sib_send)
+    landed(xi.at[pl.ds(0, PEERS)], i_send)
+    landed(part, g_send)
 
 
 def local(images, texts, loss_weights):
@@ -152,24 +154,22 @@
     dma = pltpu.SemaphoreType.DMA
     grads = pl.pallas_call(
         functools.partial(kernel, scale),
-        out_shape=jax.ShapeDtypeStruct((2, count, width), jnp.float32),
-        in_specs=[pl.BlockSpec(memory_space=pl.ANY)] * 3,
+        out_shape=pltpu.VMEM((2, count, width), jnp.float32),
+        in_specs=[pl.BlockSpec(memory_space=pltpu.HBM)] * 3,
         out_specs=pl.BlockSpec(memory_space=pltpu.VMEM),
         scratch_shapes=[
             pltpu.SMEM((2,), jnp.float32),
-            pltpu.VMEM((count, width), jnp.bfloat16),
-            pltpu.VMEM((count, width), jnp.bfloat16),
+            pltpu.VMEM((2, count, width), jnp.bfloat16),
             pltpu.VMEM((PEERS + 1, rows, width), jnp.bfloat16),
             pltpu.VMEM((2 * NZ, rows, width), jnp.bfloat16),
             pltpu.VMEM(((PEERS + 1) * rows, 2 * NZ * rows), jnp.bfloat16),
             pltpu.VMEM((PEERS, rows, width), jnp.bfloat16),
             pltpu.VMEM((PEERS, rows, width), jnp.bfloat16),
             dma((3,)),
-            dma((len(HOPS),)), dma((len(HOPS),)),
-            dma((NZ,)), dma((NZ,)),
-            dma((PEERS,)), dma((PEERS,)), dma((PEERS,)), dma((PEERS,)),
+            dma, dma((len(GROUPS),)),
+            dma, dma, dma, dma, dma, dma,
         ],
-        compiler_params=pltpu.CompilerParams(collective_id=0, has_side_effects=True),
+        compiler_params=pltpu.CompilerParams(collective_id=0, has_side_effects=True, vmem_limit_bytes=60 * 1024 * 1024),
     )(loss_weights, images, texts)
     return (grads[0], grads[1])
 

time: 43 us -> 40.5 us (0.942)
  Pallas kernels: 40.7 us -> 39 us
  local copies, waits for them, and re-layouts: 1.4 us -> 0.63 us
    pallas_call x1, Pallas kernels: 40.7 us -> 39 us  [local(): pl.pallas_call(functools.partial(kernel, scale), out_shape=pltpu.VMEM((2,...]
    squeeze x1, local copies, waits for them, and re-layouts: 1.4 us -> 0.63 us  [local(): return (grads[0], grads[1])]
where the time goes in v3:
time: 40.5 us; the launch traced here: 40.3 us
  Pallas kernels  39 us (96%)
  between operations  0.64 us (2%)
  local copies, waits for them, and re-layouts  0.63 us (2%)
    pallas_call x1, Pallas kernels, local(): pl.pallas_call(functools.partial(kernel, scale), out_shape=pltpu.VMEM((2,...  39 us

profile of v3, /device:TPU:1, one launch (start us, length us, event | category | flops | bytes accessed | tf_op | source)
XLA Modules:
  0.0 40.3 jit_solution(12371807417787792616)
XLA Ops:
  0.6 39.0 %shard_map.50 = f32[2,8,1024]{2,1,0:T(8,128)S(1)} custom-call(f32[2]{0:T(128)} %weights_hbm.1, bf16[8,1024]{1,0:T(8,128)(2,1)} %img_hbm.1, bf16[8,1024]{1,0:T(8,128)(2,1)} %txt_hbm.1), custom_call_target="tpu_custom_call" | custom-call | tf_op jit(solution)/shard_map/pallas_call | solution.py:155
  39.7 0.6 %slice_bitcast_fusion = (f32[8,1024]{1,0:T(8,128)}, f32[8,1024]{1,0:T(8,128)}) fusion(f32[2,8,1024]{2,1,0:T(8,128)S(1)} %shard_map.50), kind=kLoop, calls=%fused_computation | loop fusion | bytes 131072 | tf_op jit(solution)/shard_map/squeeze | solution.py:174

commit v4 on v3

--- a/solution.py
+++ b/solution.py
@@ -11,6 +11,7 @@
 MESH = pl.DeviceIdType.MESH
 NX, NY, NZ, CORES = 4, 4, 16, 2
 HALF = NZ // 2
+EARLY = NZ // 2
 
 
 def ring_distance(step, size):
@@ -32,7 +33,7 @@
 GROUPS = [group[0] for group in ARRIVALS]
 
 
-def kernel(scale, weights_hbm, img_hbm, txt_hbm, out, weights, own, xi, xj, w, part, inbox, load_sem, z_send, z_recv, sib_send, sib_recv, i_send, i_recv, g_send, g_recv):
+def kernel(scale, weights_hbm, img_hbm, txt_hbm, out, weights, own, xi, xj, w, part, inbox, entered, load_sem, z_send, z_recv, sib_send, sib_recv, i_send, i_recv, g_send, g_recv):
     rows, width = xi.shape[1:]
     half = width // 2
     row, col = lax.axis_index("row"), lax.axis_index("col")
@@ -49,8 +50,15 @@
     behind = [device((x + NX - dx) % NX, (y + NY - dy) % NY, z, core) for dx, dy in PLANE[:PEERS]]
 
     barrier = pltpu.get_barrier_semaphore()
-    for peer in list(line.values()) + [sibling] + ahead:
+    late = z // EARLY
+    far_late = {d: ((z + d + NZ) % NZ) // EARLY for d in LINE_PEERS}
+    late_peers = sum(far_late.values())
+    for peer in [sibling] + ahead:
         pl.semaphore_signal(barrier, inc=1, device_id=peer, device_id_type=MESH)
+    for d in LINE_PEERS:
+        @pl.when(late * (1 - far_late[d]) == 0)
+        def _():
+            pl.semaphore_signal(barrier, inc=1, device_id=line[d], device_id_type=MESH)
 
     loads = [
         pltpu.make_async_copy(img_hbm, own.at[0], load_sem.at[0]),
@@ -64,7 +72,11 @@
     block = own[...].astype(jnp.float32).reshape(rows, width).astype(jnp.bfloat16)
     xj[0] = block
     xi[PEERS] = block
-    pl.semaphore_wait(barrier, len(line) + 1 + PEERS)
+    pl.semaphore_wait(barrier, len(line) + 1 + PEERS - (1 - late) * late_peers)
+    for d in LINE_PEERS:
+        @pl.when(late * (1 - far_late[d]) == 1)
+        def _():
+            pl.semaphore_signal(entered, inc=1, device_id=line[d], device_id_type=MESH)
 
     def hop(origin, step):
         src, dst = origin % NZ, (origin + step) % NZ
@@ -92,12 +104,17 @@
     def landed(ref, sem):
         pltpu.make_async_copy(ref, ref, sem).wait()
 
-    for origin, step in HOPS:
-        if origin == 0:
-            hop(0, step).start()
+    def begin(waiting):
+        for origin, step in HOPS:
+            if origin == 0:
+                pl.when((1 - late) * far_late[step] == waiting)(lambda step=step: hop(0, step).start())
+
+    begin(0)
     across(0).start()
     for k in range(PEERS):
         spread(k).start()
+    pl.when(late == 0)(lambda: pl.semaphore_wait(entered, late_peers))
+    begin(1)
     for group in ARRIVALS:
         landed(xj.at[pl.ds(0, len(group))] if group[0] != (5, 3) else xj.at[0], z_recv.at[GROUPS.index(group[0])])
         for origin, step in group:
@@ -165,6 +182,7 @@
             pltpu.VMEM(((PEERS + 1) * rows, 2 * NZ * rows), jnp.bfloat16),
             pltpu.VMEM((PEERS, rows, width), jnp.bfloat16),
             pltpu.VMEM((PEERS, rows, width), jnp.bfloat16),
+            pltpu.SemaphoreType.REGULAR,
             dma((3,)),
             dma, dma((len(GROUPS),)),
             dma, dma, dma, dma, dma, dma,

time: 40.5 us -> 42.6 us (1.052)
  Pallas kernels: 39 us -> 41.2 us
    pallas_call x1, Pallas kernels: 39 us -> 41.2 us  [local(): pl.pallas_call(functools.partial(kernel, scale), out_shape=pltpu.VMEM((2,...]
where the time goes in v4:
time: 42.6 us; the launch traced here: 42.4 us
  Pallas kernels  41.2 us (97%)
  between operations  0.64 us (2%)
  local copies, waits for them, and re-layouts  0.63 us (1%)
    pallas_call x1, Pallas kernels, local(): pl.pallas_call(functools.partial(kernel, scale), out_shape=pltpu.VMEM((2,...  41.2 us

profile of v4, /device:TPU:1, one launch (start us, length us, event | category | flops | bytes accessed | tf_op | source)
XLA Modules:
  0.0 42.4 jit_solution(9435378490630324222)
XLA Ops:
  0.6 41.2 %shard_map.50 = f32[2,8,1024]{2,1,0:T(8,128)S(1)} custom-call(f32[2]{0:T(128)} %weights_hbm.1, bf16[8,1024]{1,0:T(8,128)(2,1)} %img_hbm.1, bf16[8,1024]{1,0:T(8,128)(2,1)} %txt_hbm.1), custom_call_target="tpu_custom_call" | custom-call | tf_op jit(solution)/shard_map/pallas_call | solution.py:172
  41.8 0.6 %slice_bitcast_fusion = (f32[8,1024]{1,0:T(8,128)}, f32[8,1024]{1,0:T(8,128)}) fusion(f32[2,8,1024]{2,1,0:T(8,128)S(1)} %shard_map.50), kind=kLoop, calls=%fused_computation | loop fusion | bytes 131072 | tf_op jit(solution)/shard_map/squeeze | solution.py:192

commit v5 on v3

--- a/solution.py
+++ b/solution.py
@@ -26,13 +26,31 @@
 NEAR = [(0, 5), (0, 2), (0, 1), (2, 1), (5, 3), (5, 2), (5, 1), (5, -1)]
 HOPS = [hop for origin, step in NEAR for hop in ((origin, step), (-origin, -step))]
 LINE_PEERS = sorted({step for _, step in HOPS})
-ARRIVALS = [[(0, 2)], [(0, -2)], [(0, 5)], [(0, -5)]] + [
-    [(origin, step), (-origin, -step)] for origin, step in [(0, 1), (2, 1), (5, 1), (5, -1), (5, 2), (5, 3)]
-]
-GROUPS = [group[0] for group in ARRIVALS]
-
-
-def kernel(scale, weights_hbm, img_hbm, txt_hbm, out, weights, own, xi, xj, w, part, inbox, load_sem, z_send, z_recv, sib_send, sib_recv, i_send, i_recv, g_send, g_recv):
+
+
+def arrivals():
+    level, order = {0: 0}, []
+    for origin, step in NEAR:
+        level[origin + step] = level[origin] + 1
+    relays = [hop for hop in NEAR if any(origin == sum(hop) for origin, _ in NEAR)]
+    for depth in sorted({level[sum(hop)] for hop in relays}):
+        for c in (1, 0):
+            for origin, step in relays:
+                if level[origin + step] == depth:
+                    order += [[(origin, step, c)], [(-origin, -step, c)]]
+    for origin, step in sorted(set(NEAR) - set(relays), key=lambda hop: level[sum(hop)]):
+        order.append([(origin, step, 1), (origin, step, 0), (-origin, -step, 1), (-origin, -step, 0)])
+    return order
+
+
+ARRIVALS = arrivals()
+
+
+def group_of(origin, step, c):
+    return next(n for n, group in enumerate(ARRIVALS) if (origin, step, c) in group)
+
+
+def kernel(scale, weights_hbm, img_hbm, txt_hbm, out, weights, own, xi, xj, w, part, inbox, load_sem, z_send, z_recv, hand_send, hand_recv, sib_send, sib_recv, i_send, i_recv, g_send, g_recv):
     rows, width = xi.shape[1:]
     half = width // 2
     row, col = lax.axis_index("row"), lax.axis_index("col")
@@ -49,8 +67,13 @@
     behind = [device((x + NX - dx) % NX, (y + NY - dy) % NY, z, core) for dx, dy in PLANE[:PEERS]]
 
     barrier = pltpu.get_barrier_semaphore()
-    for peer in list(line.values()) + [sibling] + ahead:
+    for peer in [sibling] + ahead:
         pl.semaphore_signal(barrier, inc=1, device_id=peer, device_id_type=MESH)
+
+    @pl.when(core == 1)
+    def _():
+        for peer in line.values():
+            pl.semaphore_signal(barrier, inc=1, device_id=peer, device_id_type=MESH)
 
     loads = [
         pltpu.make_async_copy(img_hbm, own.at[0], load_sem.at[0]),
@@ -62,21 +85,24 @@
     for load in loads:
         load.wait()
     block = own[...].astype(jnp.float32).reshape(rows, width).astype(jnp.bfloat16)
-    xj[0] = block
+    xj[0, core] = block
     xi[PEERS] = block
-    pl.semaphore_wait(barrier, len(line) + 1 + PEERS)
-
-    def hop(origin, step):
+    pl.semaphore_wait(barrier, core * len(line) + 1 + PEERS)
+
+    def hop(origin, step, c):
         src, dst = origin % NZ, (origin + step) % NZ
-        k = GROUPS.index((origin, step)) if (origin, step) in GROUPS else GROUPS.index((-origin, -step))
-        part = slice(None) if dst != HALF else pl.ds(0 if step > 0 else half, half)
-        return pltpu.make_async_remote_copy(
-            src_ref=xj.at[src, :, part], dst_ref=xj.at[dst, :, part], send_sem=z_send, recv_sem=z_recv.at[k],
+        lanes = slice(None) if dst != HALF else pl.ds(0 if step > 0 else half, half)
+        return pltpu.make_async_remote_copy(
+            src_ref=xj.at[src, c, :, lanes], dst_ref=xj.at[dst, c, :, lanes], send_sem=z_send, recv_sem=z_recv.at[group_of(origin, step, c)],
             device_id=line[step], device_id_type=MESH)
 
+    hand = pltpu.make_async_remote_copy(
+        src_ref=xj.at[0, core], dst_ref=xj.at[0, core], send_sem=hand_send, recv_sem=hand_recv,
+        device_id=sibling, device_id_type=MESH)
+
     def across(slot):
         return pltpu.make_async_remote_copy(
-            src_ref=xj.at[slot], dst_ref=xj.at[slot + NZ], send_sem=sib_send, recv_sem=sib_recv,
+            src_ref=xj.at[slot], dst_ref=xj.at[slot], send_sem=sib_send, recv_sem=sib_recv,
             device_id=sibling, device_id_type=MESH)
 
     def spread(k):
@@ -92,24 +118,33 @@
     def landed(ref, sem):
         pltpu.make_async_copy(ref, ref, sem).wait()
 
-    for origin, step in HOPS:
-        if origin == 0:
-            hop(0, step).start()
-    across(0).start()
+    def begin(c):
+        for origin, step in HOPS:
+            if origin == 0:
+                hop(0, step, c).start()
+
+    pl.when(core == 1)(lambda: begin(1))
+    hand.start()
     for k in range(PEERS):
         spread(k).start()
-    for group in ARRIVALS:
-        landed(xj.at[pl.ds(0, len(group))] if group[0] != (5, 3) else xj.at[0], z_recv.at[GROUPS.index(group[0])])
-        for origin, step in group:
-            here = origin + step
-            for onward in HOPS:
-                if onward[0] == here:
-                    hop(*onward).start()
-            if abs(here) != HALF:
-                across(here % NZ).start()
-    across(HALF).start()
+    hand.wait_recv()
+
+    @pl.when(core == 1)
+    def _():
+        begin(0)
+        for n, group in enumerate(ARRIVALS):
+            landed(xj.at[0, pl.ds(0, 1)] if len(group) == 1 else xj.at[0] if sum(group[0][:2]) == HALF else xj.at[pl.ds(0, 2)], z_recv.at[n])
+            for origin, step, c in group:
+                here = origin + step
+                for onward in HOPS:
+                    if onward[0] == here:
+                        hop(*onward, c).start()
+                if c == 0 and abs(here) != HALF:
+                    across(here % NZ).start()
+        across(HALF).start()
+
     landed(xi.at[pl.ds(0, PEERS)], i_recv)
-    landed(xj.at[pl.ds(NZ, NZ)], sib_recv)
+    pl.when(core == 0)(lambda: landed(xj.at[pl.ds(1, NZ - 1)], sib_recv))
 
     blocks = PEERS + 1
     keys = xj[...].reshape(2 * NZ * rows, width)
@@ -140,8 +175,12 @@
     out[0] = mine[:8]
     out[1] = mine[8:]
 
-    landed(xj.at[pl.ds(0, NZ - 1)], z_send)
-    landed(xj.at[pl.ds(0, NZ)], sib_send)
+    @pl.when(core == 1)
+    def _():
+        landed(xj.at[pl.ds(0, NZ - 1)], z_send)
+        landed(xj.at[pl.ds(1, NZ - 1)], sib_send)
+
+    hand.wait_send()
     landed(xi.at[pl.ds(0, PEERS)], i_send)
     landed(part, g_send)
 
@@ -161,13 +200,13 @@
             pltpu.SMEM((2,), jnp.float32),
             pltpu.VMEM((2, count, width), jnp.bfloat16),
             pltpu.VMEM((PEERS + 1, rows, width), jnp.bfloat16),
-            pltpu.VMEM((2 * NZ, rows, width), jnp.bfloat16),
+            pltpu.VMEM((NZ, CORES, rows, width), jnp.bfloat16),
             pltpu.VMEM(((PEERS + 1) * rows, 2 * NZ * rows), jnp.bfloat16),
             pltpu.VMEM((PEERS, rows, width), jnp.bfloat16),
             pltpu.VMEM((PEERS, rows, width), jnp.bfloat16),
             dma((3,)),
-            dma, dma((len(GROUPS),)),
-            dma, dma, dma, dma, dma, dma,
+            dma, dma((len(ARRIVALS),)),
+            dma, dma, dma, dma, dma, dma, dma, dma,
         ],
         compiler_params=pltpu.CompilerParams(collective_id=0, has_side_effects=True, vmem_limit_bytes=60 * 1024 * 1024),
     )(loss_weights, images, texts)

time: 40.5 us -> 37.9 us (0.936)
  Pallas kernels: 39 us -> 36.3 us
    pallas_call x1, Pallas kernels: 39 us -> 36.3 us  [local(): pl.pallas_call(functools.partial(kernel, scale), out_shape=pltpu.VMEM((2,...]
where the time goes in v5:
time: 37.9 us; the launch traced here: 37.6 us
  Pallas kernels  36.3 us (96%)
  between operations  0.64 us (2%)
  local copies, waits for them, and re-layouts  0.63 us (2%)
    pallas_call x1, Pallas kernels, local(): pl.pallas_call(functools.partial(kernel, scale), out_shape=pltpu.VMEM((2,...  36.3 us

profile of v5, /device:TPU:1, one launch (start us, length us, event | category | flops | bytes accessed | tf_op | source)
XLA Modules:
  0.0 37.6 jit_solution(10810736224503319472)
XLA Ops:
  0.6 36.3 %shard_map.50 = f32[2,8,1024]{2,1,0:T(8,128)S(1)} custom-call(f32[2]{0:T(128)} %weights_hbm.1, bf16[8,1024]{1,0:T(8,128)(2,1)} %img_hbm.1, bf16[8,1024]{1,0:T(8,128)(2,1)} %txt_hbm.1), custom_call_target="tpu_custom_call" | custom-call | tf_op jit(solution)/shard_map/pallas_call | solution.py:194
  36.9 0.6 %slice_bitcast_fusion = (f32[8,1024]{1,0:T(8,128)}, f32[8,1024]{1,0:T(8,128)}) fusion(f32[2,8,1024]{2,1,0:T(8,128)S(1)} %shard_map.50), kind=kLoop, calls=%fused_computation | loop fusion | bytes 131072 | tf_op jit(solution)/shard_map/squeeze | solution.py:213

commit v6 on v5

--- a/solution.py
+++ b/solution.py
@@ -11,6 +11,7 @@
 MESH = pl.DeviceIdType.MESH
 NX, NY, NZ, CORES = 4, 4, 16, 2
 HALF = NZ // 2
+ROUNDS = NX // 2 + NY // 2 - 1
 
 
 def ring_distance(step, size):
@@ -23,7 +24,7 @@
 )
 PEERS = len(PLANE) - 1
 
-NEAR = [(0, 5), (0, 2), (0, 1), (2, 1), (5, 3), (5, 2), (5, 1), (5, -1)]
+NEAR = [(0, 3), (0, 1), (3, 2), (3, 1), (3, -1), (5, 3), (5, 2), (5, 1)]
 HOPS = [hop for origin, step in NEAR for hop in ((origin, step), (-origin, -step))]
 LINE_PEERS = sorted({step for _, step in HOPS})
 
@@ -50,7 +51,7 @@
     return next(n for n, group in enumerate(ARRIVALS) if (origin, step, c) in group)
 
 
-def kernel(scale, weights_hbm, img_hbm, txt_hbm, out, weights, own, xi, xj, w, part, inbox, load_sem, z_send, z_recv, hand_send, hand_recv, sib_send, sib_recv, i_send, i_recv, g_send, g_recv):
+def kernel(scale, weights_hbm, img_hbm, txt_hbm, out, weights, own, xi, xj, w, part, inbox, news, load_sem, z_send, z_recv, hand_send, hand_recv, sib_send, sib_recv, i_send, i_recv, g_send, g_recv):
     rows, width = xi.shape[1:]
     half = width // 2
     row, col = lax.axis_index("row"), lax.axis_index("col")
@@ -63,17 +64,9 @@
 
     sibling = device(x, y, z, 1 - core)
     line = {d: device(x, y, (z + d + NZ) % NZ, core) for d in LINE_PEERS}
-    ahead = [device((x + dx) % NX, (y + dy) % NY, z, core) for dx, dy in PLANE[:PEERS]]
+    ahead = [[device((x + dx) % NX, (y + dy) % NY, z, c) for dx, dy in PLANE[:PEERS]] for c in range(CORES)]
+    beside = [[device((x + dx) % NX, (y + dy) % NY, z, c) for dx, dy in [(1, 0), (NX - 1, 0), (0, 1), (0, NY - 1)]] for c in range(CORES)]
     behind = [device((x + NX - dx) % NX, (y + NY - dy) % NY, z, core) for dx, dy in PLANE[:PEERS]]
-
-    barrier = pltpu.get_barrier_semaphore()
-    for peer in [sibling] + ahead:
-        pl.semaphore_signal(barrier, inc=1, device_id=peer, device_id_type=MESH)
-
-    @pl.when(core == 1)
-    def _():
-        for peer in line.values():
-            pl.semaphore_signal(barrier, inc=1, device_id=peer, device_id_type=MESH)
 
     loads = [
         pltpu.make_async_copy(img_hbm, own.at[0], load_sem.at[0]),
@@ -82,12 +75,22 @@
     ]
     for load in loads:
         load.start()
+
+    barrier = pltpu.get_barrier_semaphore()
+    for peer in [sibling] + beside[1]:
+        pl.semaphore_signal(barrier, inc=1, device_id=peer, device_id_type=MESH)
+
+    @pl.when(core == 1)
+    def _():
+        for peer in line.values():
+            pl.semaphore_signal(barrier, inc=1, device_id=peer, device_id_type=MESH)
+
     for load in loads:
         load.wait()
     block = own[...].astype(jnp.float32).reshape(rows, width).astype(jnp.bfloat16)
     xj[0, core] = block
     xi[PEERS] = block
-    pl.semaphore_wait(barrier, core * len(line) + 1 + PEERS)
+    pl.semaphore_wait(barrier, core * (len(line) + 2 * len(beside[1])) + 1)
 
     def hop(origin, step, c):
         src, dst = origin % NZ, (origin + step) % NZ
@@ -105,10 +108,10 @@
             src_ref=xj.at[slot], dst_ref=xj.at[slot], send_sem=sib_send, recv_sem=sib_recv,
             device_id=sibling, device_id_type=MESH)
 
-    def spread(k):
-        return pltpu.make_async_remote_copy(
-            src_ref=xi.at[PEERS], dst_ref=xi.at[k], send_sem=i_send, recv_sem=i_recv,
-            device_id=ahead[k], device_id_type=MESH)
+    def spread(k, c):
+        return pltpu.make_async_remote_copy(
+            src_ref=xj.at[0, c], dst_ref=xi.at[k], send_sem=i_send, recv_sem=i_recv,
+            device_id=ahead[c][k], device_id_type=MESH)
 
     def give(k):
         return pltpu.make_async_remote_copy(
@@ -123,11 +126,25 @@
             if origin == 0:
                 hop(0, step, c).start()
 
+    def spread_to(distance):
+        for k, (dx, dy) in enumerate(PLANE[:PEERS]):
+            if ring_distance(dx, NX) + ring_distance(dy, NY) == distance:
+                for c in range(CORES):
+                    spread(k, c).start()
+
+    hand.start()
     pl.when(core == 1)(lambda: begin(1))
-    hand.start()
-    for k in range(PEERS):
-        spread(k).start()
     hand.wait_recv()
+
+    @pl.when(core == 0)
+    def _():
+        for n in range(ROUNDS + 1):
+            if n > 0:
+                pl.semaphore_wait(news.at[n - 1], len(beside[0]))
+            if n < ROUNDS:
+                for peer in beside[0]:
+                    pl.semaphore_signal(news.at[n], inc=1, device_id=peer, device_id_type=MESH)
+            spread_to(n + 1)
 
     @pl.when(core == 1)
     def _():
@@ -181,7 +198,11 @@
         landed(xj.at[pl.ds(1, NZ - 1)], sib_send)
 
     hand.wait_send()
-    landed(xi.at[pl.ds(0, PEERS)], i_send)
+
+    @pl.when(core == 0)
+    def _():
+        landed(xj.at[pl.ds(0, PEERS)], i_send)
+
     landed(part, g_send)
 
 
@@ -204,6 +225,7 @@
             pltpu.VMEM(((PEERS + 1) * rows, 2 * NZ * rows), jnp.bfloat16),
             pltpu.VMEM((PEERS, rows, width), jnp.bfloat16),
             pltpu.VMEM((PEERS, rows, width), jnp.bfloat16),
+            pltpu.SemaphoreType.REGULAR((ROUNDS,)),
             dma((3,)),
             dma, dma((len(ARRIVALS),)),
             dma, dma, dma, dma, dma, dma, dma, dma,

time: 37.9 us -> 37.1 us (0.979)
  Pallas kernels: 36.3 us -> 35.6 us
    pallas_call x1, Pallas kernels: 36.3 us -> 35.6 us  [local(): pl.pallas_call(functools.partial(kernel, scale), out_shape=pltpu.VMEM((2,...]
where the time goes in v6:
time: 37.1 us; the launch traced here: 36.9 us
  Pallas kernels  35.6 us (96%)
  between operations  0.64 us (2%)
  local copies, waits for them, and re-layouts  0.63 us (2%)
    pallas_call x1, Pallas kernels, local(): pl.pallas_call(functools.partial(kernel, scale), out_shape=pltpu.VMEM((2,...  35.6 us

profile of v6, /device:TPU:1, one launch (start us, length us, event | category | flops | bytes accessed | tf_op | source)
XLA Modules:
  0.0 36.9 jit_solution(18360696054845026456)
XLA Ops:
  0.6 35.6 %shard_map.50 = f32[2,8,1024]{2,1,0:T(8,128)S(1)} custom-call(f32[2]{0:T(128)} %weights_hbm.1, bf16[8,1024]{1,0:T(8,128)(2,1)} %img_hbm.1, bf16[8,1024]{1,0:T(8,128)(2,1)} %txt_hbm.1), custom_call_target="tpu_custom_call" | custom-call | tf_op jit(solution)/shard_map/pallas_call | solution.py:215
  36.2 0.6 %slice_bitcast_fusion = (f32[8,1024]{1,0:T(8,128)}, f32[8,1024]{1,0:T(8,128)}) fusion(f32[2,8,1024]{2,1,0:T(8,128)S(1)} %shard_map.50), kind=kLoop, calls=%fused_computation | loop fusion | bytes 131072 | tf_op jit(solution)/shard_map/squeeze | solution.py:235

commit v7 on v6

--- a/solution.py
+++ b/solution.py
@@ -11,7 +11,6 @@
 MESH = pl.DeviceIdType.MESH
 NX, NY, NZ, CORES = 4, 4, 16, 2
 HALF = NZ // 2
-ROUNDS = NX // 2 + NY // 2 - 1
 
 
 def ring_distance(step, size):
@@ -24,7 +23,12 @@
 )
 PEERS = len(PLANE) - 1
 
-NEAR = [(0, 3), (0, 1), (3, 2), (3, 1), (3, -1), (5, 3), (5, 2), (5, 1)]
+
+def at_distance(distance):
+    return [k for k, (dx, dy) in enumerate(PLANE) if ring_distance(dx, NX) + ring_distance(dy, NY) == distance]
+
+
+NEAR = [(0, 3), (0, 1), (3, 3), (3, -1), (3, 1), (6, 2), (6, 1), (6, -1)]
 HOPS = [hop for origin, step in NEAR for hop in ((origin, step), (-origin, -step))]
 LINE_PEERS = sorted({step for _, step in HOPS})
 
@@ -47,6 +51,12 @@
 ARRIVALS = arrivals()
 
 
+def urgent(hop):
+    last = max(NEAR, key=lambda other: abs(sum(other)))[0]
+    up = hop if hop in NEAR else (-hop[0], -hop[1])
+    return any(origin == sum(up) for origin, _ in NEAR) or up[0] == last
+
+
 def group_of(origin, step, c):
     return next(n for n, group in enumerate(ARRIVALS) if (origin, step, c) in group)
 
@@ -121,43 +131,57 @@
     def landed(ref, sem):
         pltpu.make_async_copy(ref, ref, sem).wait()
 
-    def begin(c):
-        for origin, step in HOPS:
-            if origin == 0:
-                hop(0, step, c).start()
+    def start(here, c, first):
+        for onward in HOPS:
+            if onward[0] == here and urgent(onward) == first:
+                hop(*onward, c).start()
+
+    second = at_distance(2)
 
     def spread_to(distance):
-        for k, (dx, dy) in enumerate(PLANE[:PEERS]):
-            if ring_distance(dx, NX) + ring_distance(dy, NY) == distance:
-                for c in range(CORES):
-                    spread(k, c).start()
+        for k in at_distance(distance):
+            for c in range(CORES):
+                spread(k, c).start()
 
     hand.start()
-    pl.when(core == 1)(lambda: begin(1))
+
+    @pl.when(core == 1)
+    def _():
+        for peer in beside[0]:
+            pl.semaphore_signal(news.at[0], inc=1, device_id=peer, device_id_type=MESH)
+        start(0, 1, True)
+
     hand.wait_recv()
 
     @pl.when(core == 0)
     def _():
-        for n in range(ROUNDS + 1):
-            if n > 0:
-                pl.semaphore_wait(news.at[n - 1], len(beside[0]))
-            if n < ROUNDS:
-                for peer in beside[0]:
-                    pl.semaphore_signal(news.at[n], inc=1, device_id=peer, device_id_type=MESH)
-            spread_to(n + 1)
-
-    @pl.when(core == 1)
-    def _():
-        begin(0)
+        spread_to(1)
+        pl.semaphore_wait(news.at[0], len(beside[0]))
+        for k in second:
+            pl.semaphore_signal(news.at[1], inc=1, device_id=ahead[0][k], device_id_type=MESH)
+        spread_to(2)
+        pl.semaphore_wait(news.at[1], len(second))
+        spread_to(4)
+        spread_to(3)
+
+    @pl.when(core == 1)
+    def _():
+        start(0, 0, True)
+        start(0, 1, False)
+        start(0, 0, False)
+        left = []
         for n, group in enumerate(ARRIVALS):
             landed(xj.at[0, pl.ds(0, 1)] if len(group) == 1 else xj.at[0] if sum(group[0][:2]) == HALF else xj.at[pl.ds(0, 2)], z_recv.at[n])
             for origin, step, c in group:
                 here = origin + step
-                for onward in HOPS:
-                    if onward[0] == here:
-                        hop(*onward, c).start()
+                start(here, c, True)
+                left.append((here, c))
                 if c == 0 and abs(here) != HALF:
                     across(here % NZ).start()
+            if len(group) == 1 and group[0][1] < 0 and group[0][2] == 0:
+                for here, c in left:
+                    start(here, c, False)
+                left = []
         across(HALF).start()
 
     landed(xi.at[pl.ds(0, PEERS)], i_recv)
@@ -225,7 +249,7 @@
             pltpu.VMEM(((PEERS + 1) * rows, 2 * NZ * rows), jnp.bfloat16),
             pltpu.VMEM((PEERS, rows, width), jnp.bfloat16),
             pltpu.VMEM((PEERS, rows, width), jnp.bfloat16),
-            pltpu.SemaphoreType.REGULAR((ROUNDS,)),
+            pltpu.SemaphoreType.REGULAR((2,)),
             dma((3,)),
             dma, dma((len(ARRIVALS),)),
             dma, dma, dma, dma, dma, dma, dma, dma,

time: 37.1 us -> 36.8 us (level)
  no operation moved by 1% of the time
where the time goes in v7:
time: 36.8 us; the launch traced here: 36.6 us
  Pallas kernels  35.3 us (96%)
  between operations  0.64 us (2%)
  local copies, waits for them, and re-layouts  0.63 us (2%)
    pallas_call x1, Pallas kernels, local(): pl.pallas_call(functools.partial(kernel, scale), out_shape=pltpu.VMEM((2,...  35.3 us

profile of v7, /device:TPU:1, one launch (start us, length us, event | category | flops | bytes accessed | tf_op | source)
XLA Modules:
  0.0 36.6 jit_solution(318534173436737970)
XLA Ops:
  0.6 35.3 %shard_map.50 = f32[2,8,1024]{2,1,0:T(8,128)S(1)} custom-call(f32[2]{0:T(128)} %weights_hbm.1, bf16[8,1024]{1,0:T(8,128)(2,1)} %img_hbm.1, bf16[8,1024]{1,0:T(8,128)(2,1)} %txt_hbm.1), custom_call_target="tpu_custom_call" | custom-call | tf_op jit(solution)/shard_map/pallas_call | solution.py:239
  36.0 0.6 %slice_bitcast_fusion = (f32[8,1024]{1,0:T(8,128)}, f32[8,1024]{1,0:T(8,128)}) fusion(f32[2,8,1024]{2,1,0:T(8,128)S(1)} %shard_map.50), kind=kLoop, calls=%fused_computation | loop fusion | bytes 131072 | tf_op jit(solution)/shard_map/squeeze | solution.py:259

commit v8 on v7

--- a/solution.py
+++ b/solution.py
@@ -22,6 +22,7 @@
     key=lambda o: -(ring_distance(o[0], NX) + ring_distance(o[1], NY)),
 )
 PEERS = len(PLANE) - 1
+SHARE = 5
 
 
 def at_distance(distance):
@@ -61,7 +62,7 @@
     return next(n for n, group in enumerate(ARRIVALS) if (origin, step, c) in group)
 
 
-def kernel(scale, weights_hbm, img_hbm, txt_hbm, out, weights, own, xi, xj, w, part, inbox, news, load_sem, z_send, z_recv, hand_send, hand_recv, sib_send, sib_recv, i_send, i_recv, g_send, g_recv):
+def kernel(scale, weights_hbm, img_hbm, txt_hbm, out, weights, own, xi, xj, part, inbox, news, load_sem, z_send, z_recv, hand_send, hand_recv, sib_send, sib_recv, i_send, i_recv, g_send, g_recv):
     rows, width = xi.shape[1:]
     half = width // 2
     row, col = lax.axis_index("row"), lax.axis_index("col")
@@ -125,7 +126,7 @@
 
     def give(k):
         return pltpu.make_async_remote_copy(
-            src_ref=part.at[k], dst_ref=inbox.at[k], send_sem=g_send, recv_sem=g_recv,
+            src_ref=part.at[k], dst_ref=inbox.at[k], send_sem=g_send, recv_sem=g_recv.at[k // SHARE],
             device_id=behind[k], device_id_type=MESH)
 
     def landed(ref, sem):
@@ -187,32 +188,32 @@
     landed(xi.at[pl.ds(0, PEERS)], i_recv)
     pl.when(core == 0)(lambda: landed(xj.at[pl.ds(1, NZ - 1)], sib_recv))
 
-    blocks = PEERS + 1
     keys = xj[...].reshape(2 * NZ * rows, width)
-    scores = lax.dot_general(
-        xi[...].reshape(blocks * rows, width), keys, (((1,), (1,)), ((), ())), preferred_element_type=jnp.float32)
-    lanes = scores.shape[1]
-    lane_kind = (lax.broadcasted_iota(jnp.int32, scores.shape, 1) // 8) % 2
-    row_kind = (lax.broadcasted_iota(jnp.int32, scores.shape, 0) // 8) % 2
-    turned = jnp.where(lane_kind == 0, pltpu.roll(scores, lanes - 8, 1), pltpu.roll(scores, 8, 1))
-    turned = turned.reshape(blocks, 2, 8, lanes)
-    turned = jnp.concatenate([turned[:, 1:], turned[:, :1]], axis=1).reshape(scores.shape)
-    factor = jnp.where(lane_kind == row_kind, weights[1] * scale, weights[0] * scale)
-    w[...] = ((scores - turned) * factor).astype(jnp.bfloat16)
-
-    group = 4
-    for first in range(0, blocks, group):
-        total = jnp.dot(w[pl.ds(first * rows, group * rows), :], keys, preferred_element_type=jnp.float32)
-        for k in range(first, first + group):
+    first = 0
+    for size in (8, 8):
+        scores = lax.dot_general(
+            xi[pl.ds(first, size)].reshape(size * rows, width), keys, (((1,), (1,)), ((), ())), preferred_element_type=jnp.float32)
+        lanes = scores.shape[1]
+        lane_kind = (lax.broadcasted_iota(jnp.int32, scores.shape, 1) // 8) % 2
+        row_kind = (lax.broadcasted_iota(jnp.int32, scores.shape, 0) // 8) % 2
+        turned = jnp.where(lane_kind == 0, pltpu.roll(scores, lanes - 8, 1), pltpu.roll(scores, 8, 1))
+        turned = turned.reshape(size, 2, 8, lanes)
+        turned = jnp.concatenate([turned[:, 1:], turned[:, :1]], axis=1).reshape(scores.shape)
+        factor = jnp.where(lane_kind == row_kind, weights[1] * scale, weights[0] * scale)
+        w = ((scores - turned) * factor).astype(jnp.bfloat16)
+        total = jnp.dot(w, keys, preferred_element_type=jnp.float32)
+        for k in range(first, first + size):
             block = total[(k - first) * rows : (k - first + 1) * rows]
             if k < PEERS:
                 part[k] = block.astype(jnp.bfloat16)
                 give(k).start()
             else:
                 mine = block
-    landed(inbox, g_recv)
-    for k in range(PEERS):
-        mine = mine + inbox[k].astype(jnp.float32)
+        first += size
+    for first in range(0, PEERS, SHARE):
+        landed(inbox.at[pl.ds(first, SHARE)], g_recv.at[first // SHARE])
+        for k in range(first, first + SHARE):
+            mine = mine + inbox[k].astype(jnp.float32)
     out[0] = mine[:8]
     out[1] = mine[8:]
 
@@ -246,13 +247,12 @@
             pltpu.VMEM((2, count, width), jnp.bfloat16),
             pltpu.VMEM((PEERS + 1, rows, width), jnp.bfloat16),
             pltpu.VMEM((NZ, CORES, rows, width), jnp.bfloat16),
-            pltpu.VMEM(((PEERS + 1) * rows, 2 * NZ * rows), jnp.bfloat16),
             pltpu.VMEM((PEERS, rows, width), jnp.bfloat16),
             pltpu.VMEM((PEERS, rows, width), jnp.bfloat16),
             pltpu.SemaphoreType.REGULAR((2,)),
             dma((3,)),
             dma, dma((len(ARRIVALS),)),
-            dma, dma, dma, dma, dma, dma, dma, dma,
+            dma, dma, dma, dma, dma, dma, dma, dma((PEERS // SHARE,)),
         ],
         compiler_params=pltpu.CompilerParams(collective_id=0, has_side_effects=True, vmem_limit_bytes=60 * 1024 * 1024),
     )(loss_weights, images, texts)

time: 36.8 us -> 36.8 us (level)
  no operation moved by 1% of the time
where the time goes in v8:
time: 36.8 us; the launch traced here: 36.6 us
  Pallas kernels  35.3 us (96%)
  between operations  0.64 us (2%)
  local copies, waits for them, and re-layouts  0.63 us (2%)
    pallas_call x1, Pallas kernels, local(): pl.pallas_call(functools.partial(kernel, scale), out_shape=pltpu.VMEM((2,...  35.3 us

profile of v8, /device:TPU:1, one launch (start us, length us, event | category | flops | bytes accessed | tf_op | source)
XLA Modules:
  0.0 36.6 jit_solution(7899281811655391757)
XLA Ops:
  0.6 35.3 %shard_map.50 = f32[2,8,1024]{2,1,0:T(8,128)S(1)} custom-call(f32[2]{0:T(128)} %weights_hbm.1, bf16[8,1024]{1,0:T(8,128)(2,1)} %img_hbm.1, bf16[8,1024]{1,0:T(8,128)(2,1)} %txt_hbm.1), custom_call_target="tpu_custom_call" | custom-call | tf_op jit(solution)/shard_map/pallas_call | solution.py:240
  36.0 0.6 %slice_bitcast_fusion = (f32[8,1024]{1,0:T(8,128)}, f32[8,1024]{1,0:T(8,128)}) fusion(f32[2,8,1024]{2,1,0:T(8,128)S(1)} %shard_map.50), kind=kLoop, calls=%fused_computation | loop fusion | bytes 131072 | tf_op jit(solution)/shard_map/squeeze | solution.py:259

commit v9 on v7

--- a/solution.py
+++ b/solution.py
@@ -22,6 +22,7 @@
     key=lambda o: -(ring_distance(o[0], NX) + ring_distance(o[1], NY)),
 )
 PEERS = len(PLANE) - 1
+SHARE = 5
 
 
 def at_distance(distance):
@@ -87,13 +88,13 @@
         load.start()
 
     barrier = pltpu.get_barrier_semaphore()
+    @pl.when(core == 1)
+    def _():
+        for peer in line.values():
+            pl.semaphore_signal(barrier, inc=1, device_id=peer, device_id_type=MESH)
+
     for peer in [sibling] + beside[1]:
         pl.semaphore_signal(barrier, inc=1, device_id=peer, device_id_type=MESH)
-
-    @pl.when(core == 1)
-    def _():
-        for peer in line.values():
-            pl.semaphore_signal(barrier, inc=1, device_id=peer, device_id_type=MESH)
 
     for load in loads:
         load.wait()
@@ -125,7 +126,7 @@
 
     def give(k):
         return pltpu.make_async_remote_copy(
-            src_ref=part.at[k], dst_ref=inbox.at[k], send_sem=g_send, recv_sem=g_recv,
+            src_ref=part.at[k], dst_ref=inbox.at[k], send_sem=g_send, recv_sem=g_recv.at[k // SHARE],
             device_id=behind[k], device_id_type=MESH)
 
     def landed(ref, sem):
@@ -210,9 +211,10 @@
                 give(k).start()
             else:
                 mine = block
-    landed(inbox, g_recv)
-    for k in range(PEERS):
-        mine = mine + inbox[k].astype(jnp.float32)
+    for first in range(0, PEERS, SHARE):
+        landed(inbox.at[pl.ds(first, SHARE)], g_recv.at[first // SHARE])
+        for k in range(first, first + SHARE):
+            mine = mine + inbox[k].astype(jnp.float32)
     out[0] = mine[:8]
     out[1] = mine[8:]
 
@@ -252,7 +254,7 @@
             pltpu.SemaphoreType.REGULAR((2,)),
             dma((3,)),
             dma, dma((len(ARRIVALS),)),
-            dma, dma, dma, dma, dma, dma, dma, dma,
+            dma, dma, dma, dma, dma, dma, dma, dma((PEERS // SHARE,)),
         ],
         compiler_params=pltpu.CompilerParams(collective_id=0, has_side_effects=True, vmem_limit_bytes=60 * 1024 * 1024),
     )(loss_weights, images, texts)

time: 36.8 us -> 36.7 us (level)
  no operation moved by 1% of the time
where the time goes in v9:
time: 36.7 us; the launch traced here: 36.5 us
  Pallas kernels  35.2 us (96%)
  between operations  0.64 us (2%)
  local copies, waits for them, and re-layouts  0.63 us (2%)
    pallas_call x1, Pallas kernels, local(): pl.pallas_call(functools.partial(kernel, scale), out_shape=pltpu.VMEM((2,...  35.2 us

profile of v9, /device:TPU:1, one launch (start us, length us, event | category | flops | bytes accessed | tf_op | source)
XLA Modules:
  0.0 36.5 jit_solution(9614921318905555349)
XLA Ops:
  0.6 35.2 %shard_map.50 = f32[2,8,1024]{2,1,0:T(8,128)S(1)} custom-call(f32[2]{0:T(128)} %weights_hbm.1, bf16[8,1024]{1,0:T(8,128)(2,1)} %img_hbm.1, bf16[8,1024]{1,0:T(8,128)(2,1)} %txt_hbm.1), custom_call_target="tpu_custom_call" | custom-call | tf_op jit(solution)/shard_map/pallas_call | solution.py:241
  35.9 0.6 %slice_bitcast_fusion = (f32[8,1024]{1,0:T(8,128)}, f32[8,1024]{1,0:T(8,128)}) fusion(f32[2,8,1024]{2,1,0:T(8,128)S(1)} %shard_map.50), kind=kLoop, calls=%fused_computation | loop fusion | bytes 131072 | tf_op jit(solution)/shard_map/squeeze | solution.py:261

commit v10 on v9

--- a/solution.py
+++ b/solution.py
@@ -44,8 +44,12 @@
             for origin, step in relays:
                 if level[origin + step] == depth:
                     order += [[(origin, step, c)], [(-origin, -step, c)]]
-    for origin, step in sorted(set(NEAR) - set(relays), key=lambda hop: level[sum(hop)]):
-        order.append([(origin, step, 1), (origin, step, 0), (-origin, -step, 1), (-origin, -step, 0)])
+    leaves = [hop for hop in NEAR if hop not in relays]
+    for depth in sorted({level[sum(hop)] for hop in leaves}):
+        for c in (1, 0):
+            for origin, step in leaves:
+                if level[origin + step] == depth:
+                    order.append([(origin, step, c), (-origin, -step, c)])
     return order
 
 
@@ -114,9 +118,9 @@
         src_ref=xj.at[0, core], dst_ref=xj.at[0, core], send_sem=hand_send, recv_sem=hand_recv,
         device_id=sibling, device_id_type=MESH)
 
-    def across(slot):
-        return pltpu.make_async_remote_copy(
-            src_ref=xj.at[slot], dst_ref=xj.at[slot], send_sem=sib_send, recv_sem=sib_recv,
+    def across(slot, c):
+        return pltpu.make_async_remote_copy(
+            src_ref=xj.at[slot, c], dst_ref=xj.at[slot, c], send_sem=sib_send, recv_sem=sib_recv,
             device_id=sibling, device_id_type=MESH)
 
     def spread(k, c):
@@ -172,18 +176,17 @@
         start(0, 0, False)
         left = []
         for n, group in enumerate(ARRIVALS):
-            landed(xj.at[0, pl.ds(0, 1)] if len(group) == 1 else xj.at[0] if sum(group[0][:2]) == HALF else xj.at[pl.ds(0, 2)], z_recv.at[n])
+            landed(xj.at[0, pl.ds(0, 1)] if len(group) == 1 or sum(group[0][:2]) == HALF else xj.at[0], z_recv.at[n])
             for origin, step, c in group:
                 here = origin + step
                 start(here, c, True)
                 left.append((here, c))
-                if c == 0 and abs(here) != HALF:
-                    across(here % NZ).start()
+                if here != -HALF:
+                    across(here % NZ, c).start()
             if len(group) == 1 and group[0][1] < 0 and group[0][2] == 0:
                 for here, c in left:
                     start(here, c, False)
                 left = []
-        across(HALF).start()
 
     landed(xi.at[pl.ds(0, PEERS)], i_recv)
     pl.when(core == 0)(lambda: landed(xj.at[pl.ds(1, NZ - 1)], sib_recv))

time: 36.7 us -> 36.8 us (level)
  no operation moved by 1% of the time
where the time goes in v10:
time: 36.8 us; the launch traced here: 36.6 us
  Pallas kernels  35.4 us (96%)
  between operations  0.64 us (2%)
  local copies, waits for them, and re-layouts  0.63 us (2%)
    pallas_call x1, Pallas kernels, local(): pl.pallas_call(functools.partial(kernel, scale), out_shape=pltpu.VMEM((2,...  35.4 us

profile of v10, /device:TPU:1, one launch (start us, length us, event | category | flops | bytes accessed | tf_op | source)
XLA Modules:
  0.0 36.6 jit_solution(13736166461092475500)
XLA Ops:
  0.6 35.4 %shard_map.50 = f32[2,8,1024]{2,1,0:T(8,128)S(1)} custom-call(f32[2]{0:T(128)} %weights_hbm.1, bf16[8,1024]{1,0:T(8,128)(2,1)} %img_hbm.1, bf16[8,1024]{1,0:T(8,128)(2,1)} %txt_hbm.1), custom_call_target="tpu_custom_call" | custom-call | tf_op jit(solution)/shard_map/pallas_call | solution.py:244
  36.0 0.6 %slice_bitcast_fusion = (f32[8,1024]{1,0:T(8,128)}, f32[8,1024]{1,0:T(8,128)}) fusion(f32[2,8,1024]{2,1,0:T(8,128)S(1)} %shard_map.50), kind=kLoop, calls=%fused_computation | loop fusion | bytes 131072 | tf_op jit(solution)/shard_map/squeeze | solution.py:264
